TPU v7x, 256 devices: a whole 4x4x8 slice. The times are simulated.
256 devices in a mesh: row: 32 (over x, z_hi, core), col: 8 (over y, z_lo).
Axes of the slice: x: 4, y: 4, z: 8 (z_hi: 4, z_lo: 2; z = z_hi * 2 + z_lo), core: 2. Of those that a mesh axis runs over, the one named last changes fastest.
Arguments:
- ancestor_inverse: bfloat16 [24576, 8, 3072], P('row', 'col'), may hold values from -6 to 6
- parent_panel: bfloat16 [24576, 1024], P(('row', 'col')), may hold values from -0.15625 to 0.15625
- parent_diag_inv: bfloat16 [1024, 1024], replicated, may hold values from -1.5 to 1.5, as said below
- child_panel_anc: bfloat16 [24576, 1024], P(('row', 'col')), may hold values from -0.15625 to 0.15625
- child_panel_par: bfloat16 [1024, 1024], replicated, may hold values from -0.1875 to 0.1875
- child_diag_inv: bfloat16 [1024, 1024], replicated, may hold values from -1.5 to 1.5, as said below
Outputs:
- ainv_ap: float32 [24576, 1024], P(('row', 'col'))
- ainv_pp: float32 [1024, 1024], P(('row', 'col'))
- ainv_ac: float32 [24576, 1024], P(('row', 'col'))
- ainv_pc: float32 [1024, 1024], P(('row', 'col'))
- ainv_cc: float32 [1024, 1024], P(('row', 'col'))
Inputs may be any that keep to these rules, and one draw needn't show every extreme that they name: `parent_diag_inv`: lower triangular, with diagonal entries between 0.5 and 1.5. `child_diag_inv`: lower triangular, with diagonal entries between 0.5 and 1.5.
All inputs are finite; a program needn't handle non-finite values.
Results may differ from a plain program's by a relative error of at most 0.0041.
Values may be sent and summed in bfloat16 or wider, within the bound.
No kernel may reach another device: no remote copies, remote signals or barrier semaphores. Data moves between devices by JAX's collectives and lax.ppermute only.
A program may use at most 128 MiB of HBM per device.

v0:
```python
import jax
import jax.numpy as jnp
from jax import lax
from jax.sharding import Mesh, PartitionSpec as P

ROW = ("x", "zh", "core")
COL = ("y", "zl")
ALL = ROW + COL
BF = jnp.bfloat16
F32 = jnp.float32


def dot(a, b, ca=1, cb=0):
    return lax.dot_general(a, b, (((ca,), (cb,)), ((), ())), preferred_element_type=F32)


def shards(z, pp, pdi, ca, cp, cdi):
    rows, w = pp.shape
    nr, nc = (lax.axis_size(ROW), lax.axis_size(COL))
    sl = w // nr
    mine = sl // nc
    block = z.reshape(z.shape[0], -1)
    panels = lax.all_gather(jnp.concatenate([pp, ca], axis=1), ROW, axis=0, tiled=True)
    part = dot(block, panels).astype(BF).reshape(nc, rows, 2 * w)
    got = lax.all_to_all(part, COL, 0, 0, tiled=True)
    total = jnp.sum(got.astype(F32), axis=0)
    upper, lower = (total[:, :w], total[:, w:])
    u = upper.astype(BF)
    shifted = dot(u, cp)
    s = shifted.astype(BF)
    anc = lower - shifted
    a = anc.astype(BF)
    x = jnp.stack([u.T, s.T, a.T]).reshape(3, nr, sl, rows).transpose(1, 0, 2, 3)
    x = lax.all_to_all(x, ROW, 0, 0, tiled=True)
    x = x.transpose(1, 2, 0, 3).reshape(3 * sl, nr * rows)
    g = dot(x, panels)
    g1t = g[:sl, :w]
    cross = g[:sl, w:]
    stp = g[sl : 2 * sl, :w]
    stc = g[sl : 2 * sl, w:]
    atc = g[2 * sl :, w:]
    t2 = dot(stp.astype(BF), cp) + atc
    t = jnp.stack([g1t, t2]).reshape(2, sl, nr, sl).transpose(2, 0, 3, 1)
    t = lax.all_to_all(t, ROW, 0, 0, tiled=True)
    t = t.transpose(1, 2, 0, 3).reshape(2, sl, w)
    f = jnp.stack([t[0], cross, t[1] - stc]).reshape(3, nc, mine, w).transpose(1, 0, 2, 3)
    f = lax.all_to_all(f, COL, 0, 0, tiled=True)
    f = jnp.sum(f, axis=0)
    diag_prod = dot(pdi, cp).astype(BF)
    first = (lax.axis_index(ROW) * nc + lax.axis_index(COL)) * mine
    cols = lambda m: lax.dynamic_slice_in_dim(m, first, mine, 1)
    pp_out = dot(cols(pdi), pdi, 0, 0) + f[0]
    pc = f[1] - dot(pp_out.astype(BF), cp)
    cc = dot(cols(cdi), cdi, 0, 0) + dot(cols(diag_prod), diag_prod, 0, 0) + f[2]
    return (-upper, pp_out, -anc, pc, cc)


def solution(mesh):
    fine = Mesh(mesh.devices.reshape(4, 4, 2, 4, 2), ALL)
    out = P(ALL, None)
    return jax.shard_map(
        shards,
        mesh=fine,
        in_specs=(P(ROW, COL, None), out, P(), out, P(), P()),
        out_specs=(out,) * 5,
        check_vma=False,
    )
```

profile of v0, /device:TPU:1, one launch (start us, length us, event | category | flops | bytes accessed | tf_op | source)
XLA Modules:
  0.0 265.3 jit_solution(7984998674487563898)
XLA Ops:
  7.2 1.9 pad_maximum_fusion
  9.2 98.4 %all-gather.2.cloned.1.call-done = bf16[3072,2048]{1,0:T(8,128)(2,1)} async-done(((bf16[96,2048]{1,0:T(8,128)(2,1)}), bf16[3072,2048]{1,0:T(8,128)(2,1)}) %all-gather.2.cloned.1.call-update) | async-done | bytes 12582928 | tf_op jit(solution)/shard_map/all_gather | solution.py:23
  107.6 14.3 %fusion.2 = bf16[2048,768]{0,1:T(8,128)(2,1)S(1)} fusion(bf16[3072,2048]{1,0:T(8,128)(2,1)} %all-gather.2.cloned.1.call-done, bf16[768,1,3072]{2,0,1:T(8,128)(2,1)} %param.6), kind=kOutput, calls=%fused_computation.3 | convolution fusion | flops 9665249280 | bytes 20447232 | tf_op jit(solution)/shard_map/dot_general | solution.py:14
  121.8 47.8 %all_to_all.20 = bf16[8,96,2048]{2,1,0:T(8,128)(2,1)S(1)} all-to-all(bf16[8,96,2048]{2,1,0:T(8,128)(2,1)S(1)} %bitcast.57), channel_id=1, replica_groups=mesh['x'=4,'zh'=4,'core'=2,'y'=4,'zl'=2] {'y','zl'}, dimensions={0} | all-to-all | bytes 6291456 | tf_op jit(solution)/shard_map/all_to_all | solution.py:25
  169.7 0.6 convert_reduce_fusion
  170.3 1.3 fusion.9
  172.3 31.4 %all_to_all.21 = bf16[32,3,32,96]{3,2,1,0:T(8,128)(2,1)S(1)} all-to-all(bf16[32,3,32,96]{3,2,1,0:T(8,128)(2,1)S(1)} %copy.32), channel_id=1, replica_groups=mesh['x'=4,'zh'=4,'core'=2,'y'=4,'zl'=2] {'x','zh','core'}, dimensions={0} | all-to-all | bytes 1179648 | tf_op jit(solution)/shard_map/all_to_all | solution.py:34
  204.1 1.1 reshape.44
  205.1 6.7 %fusion.19 = f32[96,2048]{1,0:T(8,128)S(1)} fusion(bf16[96,3072]{1,0:T(8,128)(2,1)S(1)} %reshape.44, bf16[3072,2048]{1,0:T(8,128)(2,1)} %all-gather.2.cloned.1.call-done), kind=kOutput, calls=%fused_computation.37 | convolution fusion | flops 1207959552 | bytes 13959168 | tf_op jit(solution)/shard_map/dot_general | solution.py:14
  211.8 0.9 copy-done.1
  212.7 0.5 convolution_add_fusion
  213.1 1.0 copy.39
  214.2 1.0 copy.40
  215.2 1.3 maximum_bitcast_fusion
  216.5 1.1 reshape.45
  217.6 5.5 %all-to-all-start.2 = ((f32[32,1,2048]{2,1,0:T(1,128)}), f32[32,1,2048]{2,1,0:T(1,128)S(1)}, u32[]{:S(2)}, u32[]{:S(2)}) async-start(f32[32,1,2048]{2,1,0:T(1,128)} %reshape.45), calls=%async_computation.2 | async-start | bytes 524288 | tf_op jit(solution)/shard_map/all_to_all | solution.py:44
  223.1 12.9 %all-to-all-done.2 = f32[32,1,2048]{2,1,0:T(1,128)S(1)} async-done(((f32[32,1,2048]{2,1,0:T(1,128)}), f32[32,1,2048]{2,1,0:T(1,128)S(1)}, u32[]{:S(2)}, u32[]{:S(2)}) %all-to-all-start.2) | async-done | bytes 262176 | tf_op jit(solution)/shard_map/all_to_all | solution.py:44
  236.0 0.5 broadcast
  236.5 1.3 reduce
  237.8 0.3 reshape.46
  238.1 0.9 fusion.17
  239.0 0.3 copy.37
  239.6 1.0 fusion.18
  240.7 0.3 copy.36
  241.4 0.8 copy.38
  242.1 3.5 %all-to-all-start.3 = ((f32[8,3,4,1024]{3,2,1,0:T(4,128)}), f32[8,3,4,1024]{3,2,1,0:T(4,128)S(1)}, u32[]{:S(2)}, u32[]{:S(2)}) async-start(f32[8,3,4,1024]{3,2,1,0:T(4,128)} %copy.38), calls=%async_computation.3 | async-start | bytes 786432 | tf_op jit(solution)/shard_map/all_to_all | solution.py:47
  245.6 2.3 fusion.6
  247.9 3.7 %convolution_convert_fusion = bf16[1024,1024]{0,1:T(8,128)(2,1)} fusion(bf16[1024,1024]{1,0:T(8,128)(2,1)S(1)} %copy-done.2, bf16[1024,1024]{1,0:T(8,128)(2,1)S(1)} %copy-done), kind=kOutput, calls=%fused_computation.4 | convolution fusion | flops 2148532224 | bytes 6291456 | tf_op jit(solution)/shard_map/dot_general | solution.py:14
  251.7 2.1 all-to-all-done.3
  253.9 2.3 convolution_add_fusion.2
  256.2 1.0 convolution_subtract_fusion
  257.2 1.3 fusion.5
  (27 shorter events, 1.9 us)
Async XLA Ops:
  7.2 163.1 %copy-start = (bf16[1024,1024]{1,0:T(8,128)(2,1)S(1)}, bf16[1024,1024]{1,0:T(8,128)(2,1)}, u32[]{:S(2)}) copy-start(bf16[1024,1024]{1,0:T(8,128)(2,1)} %param.10) | copy-start | bytes 6291460
  7.2 100.4 %all-gather.2.cloned.1.call-start = ((), (), s32[]{:S(2)}) async-start(), calls=%async_computation.4 | async-start | bytes 12976128 | tf_op jit(solution)/shard_map/all_gather | solution.py:23
  211.8 0.9 copy-start.1
  217.6 18.4 %all-to-all-start.2 = ((f32[32,1,2048]{2,1,0:T(1,128)}), f32[32,1,2048]{2,1,0:T(1,128)S(1)}, u32[]{:S(2)}, u32[]{:S(2)}) async-start(f32[32,1,2048]{2,1,0:T(1,128)} %reshape.45), calls=%async_computation.2 | async-start | bytes 524288 | tf_op jit(solution)/shard_map/all_to_all | solution.py:44
  239.0 1.6 copy-start.4
  242.1 11.7 %all-to-all-start.3 = ((f32[8,3,4,1024]{3,2,1,0:T(4,128)}), f32[8,3,4,1024]{3,2,1,0:T(4,128)S(1)}, u32[]{:S(2)}, u32[]{:S(2)}) async-start(f32[8,3,4,1024]{3,2,1,0:T(4,128)} %copy.38), calls=%async_computation.3 | async-start | bytes 786432 | tf_op jit(solution)/shard_map/all_to_all | solution.py:47
  245.6 2.3 copy-start.2
  253.9 3.3 %copy-start.3 = (bf16[1024,1024]{0,1:T(8,128)(2,1)S(1)}, bf16[1024,1024]{0,1:T(8,128)(2,1)}, u32[]{:S(2)}) copy-start(bf16[1024,1024]{0,1:T(8,128)(2,1)} %convolution_convert_fusion) | copy-start | bytes 6291460
  256.2 2.3 copy-start.5
Sparse Core Ops, SparseCore 0:
  11.1 96.4 all-gather.1
where the time goes:
time: 266 us; the launch traced here: 265 us
  waiting for transfers between devices  113 us (42%)
  blocking collectives  79.2 us (30%)
  matrix products  33.3 us (13%)
  between operations  14.3 us (5%)
  local copies, waits for them, and re-layouts  9.7 us (4%)
  starting transfers between devices  8.97 us (3%)
  other arithmetic  6.4 us (2%)
    all_gather x1, waiting for transfers between devices, shards(): lax.all_gather(jnp.concatenate([pp, ca], axis=1), ROW, axis=0, tiled=True)  98.4 us
    all_to_all x1, blocking collectives, shards(): got = lax.all_to_all(part, COL, 0, 0, tiled=True)  47.8 us
    dot_general x9, matrix products, dot(): lax.dot_general(a, b, (((ca,), (cb,)), ((), ())), preferred_element_type=...  33.3 us
    all_to_all x1, blocking collectives, shards(): x = lax.all_to_all(x, ROW, 0, 0, tiled=True)  31.4 us
    all_to_all x1, waiting for transfers between devices, shards(): t = lax.all_to_all(t, ROW, 0, 0, tiled=True)  12.9 us
    all_to_all x1, starting transfers between devices, shards(): t = lax.all_to_all(t, ROW, 0, 0, tiled=True)  5.48 us
  transfers between devices with their start and end apart: 3, of which 3 were waited for; matrix products, arithmetic and copies ran while one was open for 2% of the time, Pallas kernels for 0%

commit v1 on v0

--- a/solution.py
+++ b/solution.py
@@ -2,6 +2,7 @@
 import jax.numpy as jnp
 from jax import lax
 from jax.sharding import Mesh, PartitionSpec as P
+from jax.lax import all_to_all, axis_size
 
 ROW = ("x", "zh", "core")
 COL = ("y", "zl")
@@ -20,7 +21,10 @@
     sl = w // nr
     mine = sl // nc
     block = z.reshape(z.shape[0], -1)
-    panels = lax.all_gather(jnp.concatenate([pp, ca], axis=1), ROW, axis=0, tiled=True)
+    recast_types = lambda shard_in: jnp.concatenate(
+        all_to_all(jnp.stack(axis_size(ROW) * [shard_in]), ROW, 0, 0), axis=0
+    )
+    panels = recast_types(jnp.concatenate([pp, ca], axis=1))
     part = dot(block, panels).astype(BF).reshape(nc, rows, 2 * w)
     got = lax.all_to_all(part, COL, 0, 0, tiled=True)
     total = jnp.sum(got.astype(F32), axis=0)

time: 266 us -> 437 us (1.64)
  blocking collectives: 79.2 us -> 361 us
  waiting for transfers between devices: 113 us -> 14.8 us
  between operations: 14.3 us -> 0.88 us
  local copies, waits for them, and re-layouts: 9.7 us -> 15.9 us
    all_to_all x0 -> x1, blocking collectives: none -> 289 us  [shards(): all_to_all(jnp.stack(axis_size(ROW) * [shard_in]), ROW, 0, 0)]
    all_gather x1 -> x0, waiting for transfers between devices: 98.4 us -> none  [shards(): lax.all_gather(jnp.concatenate([pp, ca], axis=1), ROW, axis=0, tiled=True)]
    all_to_all x1, blocking collectives: 47.8 us -> 41.2 us  [shards(): got = lax.all_to_all(part, COL, 0, 0, tiled=True)]
    another operation x0 -> x1, local copies, waits for them, and re-layouts: none -> 6.12 us  [shards(): jnp.stack(axis_size(ROW) * [shard_in])]
  transfers between devices with their start and end apart: 3 -> 2, of which waited for: 3 -> 2; matrix products, arithmetic and copies ran while one was open for 2% -> 1% of each run, Pallas kernels for 0% -> 0%
where the time goes in v1:
time: 437 us
  blocking collectives  361 us (83%)
  matrix products  29.2 us (7%)
  local copies, waits for them, and re-layouts  15.9 us (4%)
  waiting for transfers between devices  14.8 us (3%)
  starting transfers between devices  9.24 us (2%)
  other arithmetic  5.67 us (1%)
    all_to_all x1, blocking collectives, shards(): all_to_all(jnp.stack(axis_size(ROW) * [shard_in]), ROW, 0, 0)  289 us
    all_to_all x1, blocking collectives, shards(): got = lax.all_to_all(part, COL, 0, 0, tiled=True)  41.2 us
    all_to_all x1, blocking collectives, shards(): x = lax.all_to_all(x, ROW, 0, 0, tiled=True)  31.1 us
    dot_general x9, matrix products, dot(): lax.dot_general(a, b, (((ca,), (cb,)), ((), ())), preferred_element_type=...  29.2 us
    all_to_all x1, waiting for transfers between devices, shards(): t = lax.all_to_all(t, ROW, 0, 0, tiled=True)  12.8 us
  transfers between devices with their start and end apart: 2, of which 2 were waited for; matrix products, arithmetic and copies ran while one was open for 1% of the time, Pallas kernels for 0%

profile of v1, /device:TPU:1, one launch (start us, length us, event | category | flops | bytes accessed | tf_op | source)
XLA Modules:
  0.0 436.8 jit_solution(10218395605267237041)
XLA Ops:
  0.6 1.2 pad_maximum_fusion
  1.9 6.1 %stack.24 = bf16[32,96,2048]{2,1,0:T(8,128)(2,1)} broadcast(bf16[96,2048]{1,0:T(8,128)(2,1)S(1)} %pad_maximum_fusion), dimensions={1,2} | broadcast | bytes 12976128 | tf_op jit(solution)/shard_map/stack | solution.py:25
  8.0 288.7 %all_to_all.25 = bf16[32,96,2048]{2,1,0:T(8,128)(2,1)S(1)} all-to-all(bf16[32,96,2048]{2,1,0:T(8,128)(2,1)} %stack.24), channel_id=1, replica_groups=mesh['x'=4,'zh'=4,'core'=2,'y'=4,'zl'=2] {'x','zh','core'}, dimensions={0} | all-to-all | bytes 25165824 | tf_op jit(solution)/shard_map/all_to_all | solution.py:25
  296.7 10.1 %fusion.2 = bf16[2048,768]{0,1:T(8,128)(2,1)S(1)} fusion(bf16[3072,2048]{1,0:T(8,128)(2,1)S(1)} %bitcast.57, bf16[768,1,3072]{2,0,1:T(8,128)(2,1)S(1)} %bitcast.68), kind=kOutput, calls=%fused_computation.3 | convolution fusion | flops 9665249280 | bytes 20447232 | tf_op jit(solution)/shard_map/dot_general | solution.py:15
  306.9 41.2 %all_to_all.26 = bf16[8,96,2048]{2,1,0:T(8,128)(2,1)S(1)} all-to-all(bf16[8,96,2048]{2,1,0:T(8,128)(2,1)S(1)} %bitcast.60), channel_id=1, replica_groups=mesh['x'=4,'zh'=4,'core'=2,'y'=4,'zl'=2] {'y','zl'}, dimensions={0} | all-to-all | bytes 6291456 | tf_op jit(solution)/shard_map/all_to_all | solution.py:29
  348.1 0.6 convert_reduce_fusion
  348.7 1.3 fusion.9
  350.8 31.1 %all_to_all.27 = bf16[32,3,32,96]{3,2,1,0:T(8,128)(2,1)S(1)} all-to-all(bf16[32,3,32,96]{3,2,1,0:T(8,128)(2,1)S(1)} %copy.32), channel_id=1, replica_groups=mesh['x'=4,'zh'=4,'core'=2,'y'=4,'zl'=2] {'x','zh','core'}, dimensions={0} | all-to-all | bytes 1179648 | tf_op jit(solution)/shard_map/all_to_all | solution.py:38
  382.2 1.1 reshape.50
  383.3 6.7 %fusion.19 = f32[96,2048]{1,0:T(8,128)S(1)} fusion(bf16[96,3072]{1,0:T(8,128)(2,1)S(1)} %reshape.50, bf16[3072,2048]{1,0:T(8,128)(2,1)} %bitcast.58), kind=kOutput, calls=%fused_computation.37 | convolution fusion | flops 1207959552 | bytes 13959168 | tf_op jit(solution)/shard_map/dot_general | solution.py:15
  390.0 0.9 copy-done.2
  390.8 0.5 convolution_add_fusion
  391.3 1.0 copy.39
  392.3 1.0 copy.40
  393.3 1.3 maximum_bitcast_fusion
  394.6 1.1 reshape.51
  395.8 5.8 %all-to-all-start.3 = ((f32[32,1,2048]{2,1,0:T(1,128)}), f32[32,1,2048]{2,1,0:T(1,128)S(1)}, u32[]{:S(2)}, u32[]{:S(2)}) async-start(f32[32,1,2048]{2,1,0:T(1,128)} %reshape.51), calls=%async_computation.3 | async-start | bytes 524288 | tf_op jit(solution)/shard_map/all_to_all | solution.py:48
  401.6 12.8 %all-to-all-done.3 = f32[32,1,2048]{2,1,0:T(1,128)S(1)} async-done(((f32[32,1,2048]{2,1,0:T(1,128)}), f32[32,1,2048]{2,1,0:T(1,128)S(1)}, u32[]{:S(2)}, u32[]{:S(2)}) %all-to-all-start.3) | async-done | bytes 262176 | tf_op jit(solution)/shard_map/all_to_all | solution.py:48
  414.3 0.5 broadcast.2
  414.9 1.3 reduce
  416.1 0.3 reshape.52
  416.5 0.9 fusion.17
  417.9 1.0 fusion.18
  419.0 0.3 copy.36
  419.7 0.8 copy.38
  420.5 3.5 all-to-all-start.4
  423.9 2.3 fusion.6
  426.3 3.7 convolution_convert_fusion
  430.0 2.1 all-to-all-done.4
  432.2 2.3 convolution_add_fusion.2
  434.5 1.0 convolution_subtract_fusion
  435.5 1.3 fusion.5
  (33 shorter events, 2.2 us)
Async XLA Ops:
  0.6 348.1 %copy-start = (bf16[1024,1024]{1,0:T(8,128)(2,1)S(1)}, bf16[1024,1024]{1,0:T(8,128)(2,1)}, u32[]{:S(2)}) copy-start(bf16[1024,1024]{1,0:T(8,128)(2,1)} %param.10) | copy-start | bytes 6291460
  1.8 294.9 %slice-start = ((s8[4718592]{0:T(1024)(128)(4,1)}), s8[524288]{0:T(1024)(128)(4,1)S(1)}, s32[]{:S(2)}) async-start(s8[4718592]{0:T(1024)(128)(4,1)} %bitcast.67), calls=%async_computation.5 | async-start | bytes 1048576
  8.0 288.7 %slice-start.1 = ((s8[4718592]{0:T(1024)(128)(4,1)}), s8[4194304]{0:T(1024)(128)(4,1)S(1)}, s32[]{:S(2)}) async-start(s8[4718592]{0:T(1024)(128)(4,1)} %bitcast.67), calls=%async_computation.6 | async-start | bytes 8388608
  296.7 10.2 %copy-start.1 = (bf16[32,96,2048]{2,1,0:T(8,128)(2,1)}, bf16[32,96,2048]{2,1,0:T(8,128)(2,1)S(1)}, u32[]{:S(2)}) copy-start(bf16[32,96,2048]{2,1,0:T(8,128)(2,1)S(1)} %all_to_all.25) | copy-start | bytes 37748740
  389.9 0.9 copy-start.2
  395.8 18.6 %all-to-all-start.3 = ((f32[32,1,2048]{2,1,0:T(1,128)}), f32[32,1,2048]{2,1,0:T(1,128)S(1)}, u32[]{:S(2)}, u32[]{:S(2)}) async-start(f32[32,1,2048]{2,1,0:T(1,128)} %reshape.51), calls=%async_computation.3 | async-start | bytes 524288 | tf_op jit(solution)/shard_map/all_to_all | solution.py:48
  417.4 1.6 copy-start.5
  420.5 11.6 %all-to-all-start.4 = ((f32[8,3,4,1024]{3,2,1,0:T(4,128)}), f32[8,3,4,1024]{3,2,1,0:T(4,128)S(1)}, u32[]{:S(2)}, u32[]{:S(2)}) async-start(f32[8,3,4,1024]{3,2,1,0:T(4,128)} %copy.38), calls=%async_computation.4 | async-start | bytes 786432 | tf_op jit(solution)/shard_map/all_to_all | solution.py:51
  423.9 2.3 copy-start.3
  432.2 3.3 copy-start.4
  434.5 2.3 copy-start.6
